TPU v7x, 32 devices: a whole 2x2x4 slice. The times are simulated.
32 devices in a mesh: mod: 4 (over z), frm: 2 (over x), ori: 4 (over y, core).
Axes of the slice: x: 2, y: 2, z: 4, core: 2. Of those that a mesh axis runs over, the one named last changes fastest.
Arguments:
- counts: int32 [512, 128, 128], P(('frm', 'ori'), 'mod'), may hold values from 0 to 8
- slice_codes: int32 [4096, 128, 128], P('ori', ('mod', 'frm')), may hold values from 0 to 2047
- pixel_mask: int32 [128, 128], P('mod'), may hold values 0 or 1
Outputs:
- log_posterior: float32 [2, 256, 4096], P('frm', 'mod', 'ori')
All inputs are finite; a program needn't handle non-finite values. No bound on the sum of `pixel_mask` on one device may be relied on, other than what follows from the above.
Results may differ from a plain program's by a relative error of at most 0.0024.
Values may be sent and summed in bfloat16 or wider, within the bound.
A program may use at most 64 MiB of HBM per device.

v0:
```python
import math
import jax
import jax.numpy as jnp
from jax import lax
from jax.sharding import PartitionSpec as P

PASSES = 8
TIME_STEP = 0.2
EDGE_SCALE = 2.0
LOG_FLOOR = -7.0
CODE_STEP = 1.0 / 256.0


def extended(x, sides, width):
    for axis, dim in sides:
        peers, length = (lax.axis_size(axis), x.shape[dim])
        up = [(i, (i + 1) % peers) for i in range(peers - 1)]
        down = [(j, i) for i, j in up]
        last = lax.slice_in_dim(x, length - width, length, axis=dim)
        leading = lax.slice_in_dim(x, 0, width, axis=dim)
        before = lax.ppermute(last, axis, up)
        after = lax.ppermute(leading, axis, down)
        x = jnp.concatenate([before, x, after], axis=dim)
    return x


def conduct(difference):
    ratio = difference / EDGE_SCALE
    return difference / (1.0 + ratio * ratio)


def relax_once(padded):
    centre = padded[:, 1:-1, :]
    column_pad = jnp.zeros((centre.shape[0], centre.shape[1], 1), jnp.float32)
    left_side = jnp.concatenate([column_pad, centre[:, :, :-1]], axis=2)
    right_side = jnp.concatenate([centre[:, :, 1:], column_pad], axis=2)
    flux_sum = conduct(padded[:, :-2, :] - centre) + conduct(padded[:, 2:, :] - centre)
    flux_sum = flux_sum + conduct(left_side - centre) + conduct(right_side - centre)
    return centre + TIME_STEP * flux_sum


def body(counts, slice_codes, pixel_mask):
    intensity = counts.astype(jnp.float32)
    module_rows = intensity.shape[1]
    total_rows = module_rows * lax.axis_size("mod")
    first_row = lax.axis_index("mod") * module_rows
    row_ids = first_row - 1 + lax.broadcasted_iota(jnp.int32, (1, module_rows + 2, 1), 1)
    inside = ((row_ids >= 0) & (row_ids < total_rows)).astype(jnp.float32)
    for pair_index in range(PASSES // 2):
        padded = extended(intensity, (("mod", 1),), 2)
        widened = relax_once(padded) * inside
        intensity = relax_once(widened)
    cleaned = intensity.astype(jnp.bfloat16) * pixel_mask.astype(jnp.bfloat16)[None]
    gathered = lax.all_gather(cleaned, "ori", axis=0, tiled=True)
    log_slices = (LOG_FLOOR + slice_codes.astype(jnp.float32) * CODE_STEP).astype(jnp.bfloat16)
    band_rows = log_slices.shape[1]
    own_mask = lax.dynamic_slice_in_dim(
        pixel_mask, lax.axis_index("frm") * band_rows, band_rows, 0
    ).astype(jnp.float32)
    local_totals = jnp.sum(jnp.exp(log_slices.astype(jnp.float32)) * own_mask[None], axis=(1, 2))
    module_totals = lax.psum(local_totals, "frm")
    product = lax.dot_general(
        gathered,
        lax.all_gather(log_slices, "frm", axis=1, tiled=True),
        (((1, 2), (1, 2)), ((), ())),
        preferred_element_type=jnp.float32,
    )
    partial_value = product - module_totals[None, :]
    scale_factor = 1.0 / math.sqrt(module_rows * lax.axis_size("mod") * intensity.shape[2])
    summed = lax.psum(partial_value, "mod")
    share_rows = summed.shape[0] // lax.axis_size("mod")
    own_rows = lax.dynamic_slice_in_dim(summed, lax.axis_index("mod") * share_rows, share_rows, 0)
    scores = own_rows * scale_factor
    peaks = lax.pmax(jnp.max(scores, axis=1), "ori")
    masses = lax.psum(jnp.sum(jnp.exp(scores - peaks[:, None]), axis=1), "ori")
    log_posterior = scores - (peaks + jnp.log(masses))[:, None]
    return log_posterior[None]


def solution(mesh):
    in_specs = (P(("frm", "ori"), "mod", None), P("ori", ("mod", "frm"), None), P("mod", None))
    out_specs = P("frm", "mod", "ori")
    return jax.shard_map(body, mesh=mesh, in_specs=in_specs, out_specs=out_specs, check_vma=False)
```

profile of v0, /device:TPU:0, one launch (start us, length us, event | category | flops | bytes accessed | tf_op | source)
XLA Modules:
  0.0 270.0 jit_solution(14299693022543329256)
XLA Ops:
  6.5 0.0 all-gather.3.cloned.1.call-start
  6.5 1.8 copy_convert_fusion.1
  8.4 5.0 %collective-permute-start = (f32[64,2,128]{2,0,1:T(8,128)S(1)}, f32[64,2,128]{2,0,1:T(8,128)S(1)}, u32[]{:S(2)}, u32[]{:S(2)}) collective-permute-start(f32[64,2,128]{2,0,1:T(8,128)S(1)} %get-tuple-element.29), channel_id=1, source_target_pairs={{0,8},{8,16},{16,24},{1,9},{9,17},{17,25},{2,10},{10,18},{18,26},{... | collective-permute-start | bytes 196616 | tf_op jit(solution)/shard_map/ppermute | solution.py:21
  13.4 1.3 collective-permute-start.1
  14.7 0.6 collective-permute-done
  15.2 4.3 %collective-permute-done.1 = f32[64,2,128]{2,0,1:T(8,128)S(1)} collective-permute-done((f32[64,2,128]{2,0,1:T(8,128)S(1)}, f32[64,2,128]{2,0,1:T(8,128)S(1)}, u32[]{:S(2)}, u32[]{:S(2)}) %collective-permute-start.1) | collective-permute-done | bytes 65568 | tf_op jit(solution)/shard_map/ppermute | solution.py:22
  19.5 0.1 pad_maximum_fusion
  19.6 0.4 fusion.10
  20.0 1.2 add_multiply_fusion.3
  21.2 0.4 fusion.14
  21.6 1.1 multiply_add_fusion.2
  22.7 3.5 %collective-permute-start.2 = (f32[64,2,128]{2,0,1:T(8,128)S(1)}, f32[64,2,128]{2,0,1:T(8,128)S(1)}, u32[]{:S(2)}, u32[]{:S(2)}) collective-permute-start(f32[64,2,128]{2,0,1:T(8,128)S(1)} %get-tuple-element.27), channel_id=1, source_target_pairs={{0,8},{8,16},{16,24},{1,9},{9,17},{17,25},{2,10},{10,18},{18,26},{... | collective-permute-start | bytes 196616 | tf_op jit(solution)/shard_map/ppermute | solution.py:21
  26.2 1.3 collective-permute-start.3
  27.5 0.6 collective-permute-done.2
  28.1 4.3 %collective-permute-done.3 = f32[64,2,128]{2,0,1:T(8,128)S(1)} collective-permute-done((f32[64,2,128]{2,0,1:T(8,128)S(1)}, f32[64,2,128]{2,0,1:T(8,128)S(1)}, u32[]{:S(2)}, u32[]{:S(2)}) %collective-permute-start.3) | collective-permute-done | bytes 65568 | tf_op jit(solution)/shard_map/ppermute | solution.py:22
  32.4 0.1 pad_maximum_fusion.1
  32.5 0.4 fusion.9
  32.9 1.2 add_multiply_fusion.2
  34.2 0.4 fusion.13
  34.5 1.1 multiply_add_fusion.1
  35.6 3.5 %collective-permute-start.4 = (f32[64,2,128]{2,0,1:T(8,128)S(1)}, f32[64,2,128]{2,0,1:T(8,128)S(1)}, u32[]{:S(2)}, u32[]{:S(2)}) collective-permute-start(f32[64,2,128]{2,0,1:T(8,128)S(1)} %get-tuple-element.25), channel_id=1, source_target_pairs={{0,8},{8,16},{16,24},{1,9},{9,17},{17,25},{2,10},{10,18},{18,26},{... | collective-permute-start | bytes 196616 | tf_op jit(solution)/shard_map/ppermute | solution.py:21
  39.1 1.3 collective-permute-start.5
  40.4 0.6 collective-permute-done.4
  41.0 4.3 %collective-permute-done.5 = f32[64,2,128]{2,0,1:T(8,128)S(1)} collective-permute-done((f32[64,2,128]{2,0,1:T(8,128)S(1)}, f32[64,2,128]{2,0,1:T(8,128)S(1)}, u32[]{:S(2)}, u32[]{:S(2)}) %collective-permute-start.5) | collective-permute-done | bytes 65568 | tf_op jit(solution)/shard_map/ppermute | solution.py:22
  45.3 0.1 pad_maximum_fusion.2
  45.4 0.4 fusion.8
  45.8 1.2 add_multiply_fusion.1
  47.1 0.4 fusion.12
  47.4 0.0 copy-start
  47.4 1.1 multiply_add_fusion
  48.6 1.9 collective-permute-start.6
  50.5 1.5 collective-permute-start.7
  52.0 0.0 copy-done
  52.0 0.4 collective-permute-done.6
  52.4 4.3 %collective-permute-done.7 = f32[64,2,128]{2,0,1:T(8,128)S(1)} collective-permute-done((f32[64,2,128]{2,0,1:T(8,128)S(1)}, f32[64,2,128]{2,0,1:T(8,128)S(1)}, u32[]{:S(2)}, u32[]{:S(2)}) %collective-permute-start.7) | collective-permute-done | bytes 65568 | tf_op jit(solution)/shard_map/ppermute | solution.py:22
  56.6 0.1 pad_maximum_fusion.3
  56.7 0.4 fusion.7
  57.1 1.2 add_multiply_fusion
  58.4 0.4 fusion.11
  58.7 2.0 fusion.4
  60.7 0.0 all-gather.3.cloned.1.call-update
  60.7 0.0 all-gather.5.cloned.1.call-start
  60.8 7.8 %multiply_reduce_fusion = (f32[1024]{0:T(1024)S(1)}, bf16[1024,16,128]{2,0,1:T(8,128)(2,1)}) fusion(f32[16,128]{1,0:T(8,128)S(1)} %dynamic-slice_convert_fusion, s32[1024,16,128]{2,1,0:T(8,128)} %param.4), kind=kLoop, calls=%fused_computation.4 | loop fusion | flops 14679040 | bytes 12595200 | tf_op jit(solution)/shard_map/reduce_sum | solution.py:60
  68.6 0.0 all-gather.5.cloned.1.call-update
  68.6 0.0 all-reduce.18.cloned.1.call-start
  68.6 4.9 %psum.21 = f32[1024]{0:T(1024)S(1)} all-reduce(f32[1024]{0:T(1024)S(1)} %get-tuple-element.5), channel_id=1, replica_groups=mesh['mod'=4,'frm'=2,'ori'=4] {'frm'}, use_global_device_ids=true, to_apply=%region_1.0 | all-reduce | flops 1024 | bytes 8192 | tf_op jit(solution)/shard_map/psum | solution.py:61
  73.6 8.1 %all-gather.3.cloned.1.call-done = bf16[256,32,128]{2,0,1:T(8,128)(2,1)} async-done(((bf16[64,32,128]{2,0,1:T(8,128)(2,1)}), bf16[256,32,128]{2,0,1:T(8,128)(2,1)}) %all-gather.3.cloned.1.call-update) | async-done | bytes 2097168 | tf_op jit(solution)/shard_map/all_gather | solution.py:54
  81.7 105.5 %all-gather.5.cloned.1.call-done = bf16[1024,32,128]{2,0,1:T(8,128)(2,1)} async-done(((bf16[1024,16,128]{2,0,1:T(8,128)(2,1)}), bf16[1024,32,128]{2,0,1:T(8,128)(2,1)}) %all-gather.5.cloned.1.call-update) | async-done | bytes 8388624 | tf_op jit(solution)/shard_map/all_gather | solution.py:64
  187.2 7.4 %fusion.3 = f32[256,1024]{1,0:T(8,128)} fusion(bf16[256,32,128]{2,0,1:T(8,128)(2,1)} %all-gather.3.cloned.1.call-done, bf16[1024,32,128]{2,0,1:T(8,128)(2,1)} %all-gather.5.cloned.1.call-done, f32[1024]{0:T(1024)S(1)} %psum.21), kind=kOutput, calls=%fused_computation.6 | convolution fusion | flops 2147745792 | bytes 11538432 | tf_op jit(solution)/shard_map/dot_general | solution.py:62
  194.7 0.0 all-reduce.18.cloned.1.call-update
  194.7 52.1 %all-reduce.18.cloned.1.call-done = f32[256,1024]{1,0:T(8,128)} async-done(((f32[256,1024]{1,0:T(8,128)}), f32[256,1024]{1,0:T(8,128)}) %all-reduce.18.cloned.1.call-update) | async-done | bytes 1048592 | tf_op jit(solution)/shard_map/psum | solution.py:70
  246.7 1.1 fusion.5
  247.8 6.9 %pmax.7 = f32[64]{0:T(128)S(1)} all-reduce(f32[64]{0:T(128)S(1)} %fusion.5), channel_id=1, replica_groups=mesh['mod'=4,'frm'=2,'ori'=4] {'ori'}, use_global_device_ids=true, to_apply=%region_4.0 | all-reduce | flops 64 | bytes 512 | tf_op jit(solution)/shard_map/pmax | solution.py:74
  254.7 1.2 exponential_reduce_fusion
  255.8 5.9 %psum.23 = f32[64]{0:T(128)S(1)} all-reduce(f32[64]{0:T(128)S(1)} %exponential_reduce_fusion), channel_id=1, replica_groups=mesh['mod'=4,'frm'=2,'ori'=4] {'ori'}, use_global_device_ids=true, to_apply=%region_6.0 | all-reduce | flops 64 | bytes 512 | tf_op jit(solution)/shard_map/psum | solution.py:75
  261.8 1.7 subtract_bitcast_fusion
  (8 shorter events, 0.1 us)
Async XLA Ops:
  6.5 75.1 %all-gather.3.cloned.1.call-start = ((), (), s32[]{:S(2)}) async-start(), calls=%async_computation | async-start | bytes 2621440 | tf_op jit(solution)/shard_map/all_gather | solution.py:54
  8.4 6.9 %collective-permute-start = (f32[64,2,128]{2,0,1:T(8,128)S(1)}, f32[64,2,128]{2,0,1:T(8,128)S(1)}, u32[]{:S(2)}, u32[]{:S(2)}) collective-permute-start(f32[64,2,128]{2,0,1:T(8,128)S(1)} %get-tuple-element.29), channel_id=1, source_target_pairs={{0,8},{8,16},{16,24},{1,9},{9,17},{17,25},{2,10},{10,18},{18,26},{... | collective-permute-start | bytes 196616 | tf_op jit(solution)/shard_map/ppermute | solution.py:21
  13.4 6.2 %collective-permute-start.1 = (f32[64,2,128]{2,0,1:T(8,128)S(1)}, f32[64,2,128]{2,0,1:T(8,128)S(1)}, u32[]{:S(2)}, u32[]{:S(2)}) collective-permute-start(f32[64,2,128]{2,0,1:T(8,128)S(1)} %get-tuple-element.30), channel_id=1, source_target_pairs={{8,0},{16,8},{24,16},{9,1},{17,9},{25,17},{10,2},{18,10},{26,18},{... | collective-permute-start | bytes 196616 | tf_op jit(solution)/shard_map/ppermute | solution.py:22
  22.7 5.4 %collective-permute-start.2 = (f32[64,2,128]{2,0,1:T(8,128)S(1)}, f32[64,2,128]{2,0,1:T(8,128)S(1)}, u32[]{:S(2)}, u32[]{:S(2)}) collective-permute-start(f32[64,2,128]{2,0,1:T(8,128)S(1)} %get-tuple-element.27), channel_id=1, source_target_pairs={{0,8},{8,16},{16,24},{1,9},{9,17},{17,25},{2,10},{10,18},{18,26},{... | collective-permute-start | bytes 196616 | tf_op jit(solution)/shard_map/ppermute | solution.py:21
  26.2 6.2 %collective-permute-start.3 = (f32[64,2,128]{2,0,1:T(8,128)S(1)}, f32[64,2,128]{2,0,1:T(8,128)S(1)}, u32[]{:S(2)}, u32[]{:S(2)}) collective-permute-start(f32[64,2,128]{2,0,1:T(8,128)S(1)} %get-tuple-element.28), channel_id=1, source_target_pairs={{8,0},{16,8},{24,16},{9,1},{17,9},{25,17},{10,2},{18,10},{26,18},{... | collective-permute-start | bytes 196616 | tf_op jit(solution)/shard_map/ppermute | solution.py:22
  35.6 5.4 %collective-permute-start.4 = (f32[64,2,128]{2,0,1:T(8,128)S(1)}, f32[64,2,128]{2,0,1:T(8,128)S(1)}, u32[]{:S(2)}, u32[]{:S(2)}) collective-permute-start(f32[64,2,128]{2,0,1:T(8,128)S(1)} %get-tuple-element.25), channel_id=1, source_target_pairs={{0,8},{8,16},{16,24},{1,9},{9,17},{17,25},{2,10},{10,18},{18,26},{... | collective-permute-start | bytes 196616 | tf_op jit(solution)/shard_map/ppermute | solution.py:21
  39.1 6.2 %collective-permute-start.5 = (f32[64,2,128]{2,0,1:T(8,128)S(1)}, f32[64,2,128]{2,0,1:T(8,128)S(1)}, u32[]{:S(2)}, u32[]{:S(2)}) collective-permute-start(f32[64,2,128]{2,0,1:T(8,128)S(1)} %get-tuple-element.26), channel_id=1, source_target_pairs={{8,0},{16,8},{24,16},{9,1},{17,9},{25,17},{10,2},{18,10},{26,18},{... | collective-permute-start | bytes 196616 | tf_op jit(solution)/shard_map/ppermute | solution.py:22
  47.4 4.5 %copy-start = (s32[32,128]{1,0:T(8,128)S(1)}, s32[32,128]{1,0:T(8,128)}, u32[]{:S(2)}) copy-start(s32[32,128]{1,0:T(8,128)} %param.5) | copy-start | bytes 49156
  48.6 3.8 %collective-permute-start.6 = (f32[64,2,128]{2,0,1:T(8,128)S(1)}, f32[64,2,128]{2,0,1:T(8,128)S(1)}, u32[]{:S(2)}, u32[]{:S(2)}) collective-permute-start(f32[64,2,128]{2,0,1:T(8,128)S(1)} %get-tuple-element.23), channel_id=1, source_target_pairs={{0,8},{8,16},{16,24},{1,9},{9,17},{17,25},{2,10},{10,18},{18,26},{... | collective-permute-start | bytes 196616 | tf_op jit(solution)/shard_map/ppermute | solution.py:21
  50.5 6.2 %collective-permute-start.7 = (f32[64,2,128]{2,0,1:T(8,128)S(1)}, f32[64,2,128]{2,0,1:T(8,128)S(1)}, u32[]{:S(2)}, u32[]{:S(2)}) collective-permute-start(f32[64,2,128]{2,0,1:T(8,128)S(1)} %get-tuple-element.24), channel_id=1, source_target_pairs={{8,0},{16,8},{24,16},{9,1},{17,9},{25,17},{10,2},{18,10},{26,18},{... | collective-permute-start | bytes 196616 | tf_op jit(solution)/shard_map/ppermute | solution.py:22
  60.7 126.5 %all-gather.5.cloned.1.call-start = ((), (), s32[]{:S(2)}) async-start(), calls=%async_computation.1 | async-start | bytes 12582912 | tf_op jit(solution)/shard_map/all_gather | solution.py:64
  68.6 178.1 %all-reduce.18.cloned.1.call-start = ((), (), s32[]{:S(2)}) async-start(), calls=%async_computation.2 | async-start | bytes 2097152 | tf_op jit(solution)/shard_map/psum | solution.py:70
Sparse Core Ops, SparseCore 0:
  60.9 20.7 all-gather.2
  83.2 103.9 all-gather.4
  194.8 51.8 all-reduce.17
where the time goes:
time: 271 us; the launch traced here: 270 us
  waiting for transfers between devices  185 us (68%)
  other arithmetic  24.2 us (9%)
  starting transfers between devices  19.3 us (7%)
  blocking collectives  17.7 us (7%)
  between operations  13.4 us (5%)
  matrix products  7.45 us (3%)
  local copies, waits for them, and re-layouts  3.11 us (1%)
    all_gather x1, waiting for transfers between devices, body(): lax.all_gather(log_slices, 'frm', axis=1, tiled=True)  106 us
    psum x1, waiting for transfers between devices, body(): summed = lax.psum(partial_value, 'mod')  52.1 us
    ppermute x4, waiting for transfers between devices, extended(): after = lax.ppermute(leading, axis, down)  17.1 us
    ppermute x4, starting transfers between devices, extended(): before = lax.ppermute(last, axis, up)  13.8 us
    all_gather x1, waiting for transfers between devices, body(): gathered = lax.all_gather(cleaned, 'ori', axis=0, tiled=True)  8.08 us
    reduce_sum x1, other arithmetic, body(): jnp.sum(jnp.exp(log_slices.astype(jnp.float32)) * own_mask[None], axis=(1...  7.77 us
    dot_general x1, matrix products, body(): lax.dot_general(gathered, lax.all_gather(log_slices, 'frm', axis=1, tiled...  7.45 us
    pmax x1, blocking collectives, body(): peaks = lax.pmax(jnp.max(scores, axis=1), 'ori')  6.85 us
  transfers between devices with their start and end apart: 11, of which 11 were waited for; matrix products, arithmetic and copies ran while one was open for 3% of the time, Pallas kernels for 0%

commit v1 on v0

--- a/solution.py
+++ b/solution.py
@@ -9,6 +9,28 @@
 EDGE_SCALE = 2.0
 LOG_FLOOR = -7.0
 CODE_STEP = 1.0 / 256.0
+
+
+def laid_out(blocks, dim):
+    blocks = jnp.moveaxis(blocks, 0, dim)
+    shape = blocks.shape
+    return blocks.reshape(*shape[:dim], shape[dim] * shape[dim + 1], *shape[dim + 2 :])
+
+
+def grow_blocks(array, axis):
+    size = lax.axis_size(axis)
+    tiles = array[None]
+    for level in range(size.bit_length() - 1):
+        bit = 1 << level
+        other = lax.ppermute(tiles, axis, [(i, i ^ bit) for i in range(size)])
+        both = jnp.stack([tiles, other])
+        upper = lax.axis_index(axis) >> level & 1
+        tiles = jnp.where(upper == 0, both, both[::-1]).reshape(-1, *array.shape)
+    return tiles
+
+
+def collect(shard, axis, dim):
+    return laid_out(grow_blocks(shard, axis), dim)
 
 
 def extended(x, sides, width):
@@ -61,7 +83,7 @@
     module_totals = lax.psum(local_totals, "frm")
     product = lax.dot_general(
         gathered,
-        lax.all_gather(log_slices, "frm", axis=1, tiled=True),
+        collect(log_slices, "frm", 1),
         (((1, 2), (1, 2)), ((), ())),
         preferred_element_type=jnp.float32,
     )

time: 271 us -> 242 us (0.89)
  waiting for transfers between devices: 185 us -> 66.6 us
  blocking collectives: 17.7 us -> 82.7 us
  other arithmetic: 24.2 us -> 42.5 us
  starting transfers between devices: 19.3 us -> 23.4 us
    all_gather x1 -> x0, waiting for transfers between devices: 106 us -> none  [body(): lax.all_gather(log_slices, 'frm', axis=1, tiled=True)]
    psum x1, blocking collectives: 4.94 us -> 69.9 us  [body(): module_totals = lax.psum(local_totals, 'frm')]
    select_n x0 -> x1, other arithmetic: none -> 11.1 us  [grow_blocks(): tiles = jnp.where(upper == 0, both, both[::-1]).reshape(-1, *array.shape)]
    all_gather x1, waiting for transfers between devices: 8.08 us -> 0.01 us  [body(): gathered = lax.all_gather(cleaned, 'ori', axis=0, tiled=True)]
    another operation x0 -> x1, other arithmetic: none -> 7.42 us  [grow_blocks(): both = jnp.stack([tiles, other])]
    ppermute x4, waiting for transfers between devices: 17.1 us -> 12.8 us  [extended(): after = lax.ppermute(leading, axis, down)]
  transfers between devices with their start and end apart: 11 -> 11, of which waited for: 11 -> 7; matrix products, arithmetic and copies ran while one was open for 3% -> 14% of each run, Pallas kernels for 0% -> 0%
where the time goes in v1:
time: 242 us
  blocking collectives  82.7 us (34%)
  waiting for transfers between devices  66.6 us (28%)
  other arithmetic  42.5 us (18%)
  starting transfers between devices  23.4 us (10%)
  between operations  13.7 us (6%)
  matrix products  9.63 us (4%)
  local copies, waits for them, and re-layouts  3.18 us (1%)
    psum x1, blocking collectives, body(): module_totals = lax.psum(local_totals, 'frm')  69.9 us
    psum x1, waiting for transfers between devices, body(): summed = lax.psum(partial_value, 'mod')  52.1 us
    ppermute x4, starting transfers between devices, extended(): before = lax.ppermute(last, axis, up)  16.5 us
    ppermute x4, waiting for transfers between devices, extended(): after = lax.ppermute(leading, axis, down)  12.8 us
    select_n x1, other arithmetic, grow_blocks(): tiles = jnp.where(upper == 0, both, both[::-1]).reshape(-1, *array.shape)  11.1 us
    dot_general x1, matrix products, body(): lax.dot_general(gathered, collect(log_slices, 'frm', 1), (((1, 2), (1, 2)...  9.63 us
    reduce_sum x1, other arithmetic, body(): jnp.sum(jnp.exp(log_slices.astype(jnp.float32)) * own_mask[None], axis=(1...  7.48 us
    another operation x1, other arithmetic, grow_blocks(): both = jnp.stack([tiles, other])  7.42 us
  transfers between devices with their start and end apart: 11, of which 7 were waited for; matrix products, arithmetic and copies ran while one was open for 14% of the time, Pallas kernels for 0%

profile of v1, /device:TPU:0, one launch (start us, length us, event | category | flops | bytes accessed | tf_op | source)
XLA Modules:
  0.0 241.6 jit_solution(12918103787345356566)
XLA Ops:
  6.5 0.0 all-gather.2.cloned.1.call-start
  6.5 1.8 copy_convert_fusion
  8.4 5.0 %collective-permute-start = (f32[64,2,128]{2,0,1:T(8,128)S(1)}, f32[64,2,128]{2,0,1:T(8,128)S(1)}, u32[]{:S(2)}, u32[]{:S(2)}) collective-permute-start(f32[64,2,128]{2,0,1:T(8,128)S(1)} %get-tuple-element.30), channel_id=1, source_target_pairs={{0,8},{8,16},{16,24},{1,9},{9,17},{17,25},{2,10},{10,18},{18,26},{... | collective-permute-start | bytes 196616 | tf_op jit(solution)/shard_map/ppermute | solution.py:43
  13.4 1.3 collective-permute-start.1
  14.7 0.6 collective-permute-done
  15.2 4.3 %collective-permute-done.1 = f32[64,2,128]{2,0,1:T(8,128)S(1)} collective-permute-done((f32[64,2,128]{2,0,1:T(8,128)S(1)}, f32[64,2,128]{2,0,1:T(8,128)S(1)}, u32[]{:S(2)}, u32[]{:S(2)}) %collective-permute-start.1) | collective-permute-done | bytes 65568 | tf_op jit(solution)/shard_map/ppermute | solution.py:44
  19.5 0.1 pad_maximum_fusion.1
  19.6 0.4 fusion.15
  20.0 1.2 add_multiply_fusion.3
  21.2 0.4 fusion.19
  21.6 0.0 copy-start
  21.6 1.1 multiply_add_fusion.2
  22.8 3.5 %collective-permute-start.2 = (f32[64,2,128]{2,0,1:T(8,128)S(1)}, f32[64,2,128]{2,0,1:T(8,128)S(1)}, u32[]{:S(2)}, u32[]{:S(2)}) collective-permute-start(f32[64,2,128]{2,0,1:T(8,128)S(1)} %get-tuple-element.28), channel_id=1, source_target_pairs={{0,8},{8,16},{16,24},{1,9},{9,17},{17,25},{2,10},{10,18},{18,26},{... | collective-permute-start | bytes 196616 | tf_op jit(solution)/shard_map/ppermute | solution.py:43
  26.3 1.3 collective-permute-start.3
  27.6 0.0 copy-done
  27.6 0.6 collective-permute-done.2
  28.1 4.3 %collective-permute-done.3 = f32[64,2,128]{2,0,1:T(8,128)S(1)} collective-permute-done((f32[64,2,128]{2,0,1:T(8,128)S(1)}, f32[64,2,128]{2,0,1:T(8,128)S(1)}, u32[]{:S(2)}, u32[]{:S(2)}) %collective-permute-start.3) | collective-permute-done | bytes 65568 | tf_op jit(solution)/shard_map/ppermute | solution.py:44
  32.4 0.1 pad_maximum_fusion.2
  32.5 0.4 fusion.14
  32.9 0.0 slice-start
  33.0 1.2 add_multiply_fusion.2
  34.2 0.0 slice-start.1
  34.2 0.4 fusion.18
  34.6 1.1 multiply_add_fusion.1
  35.7 3.5 %collective-permute-start.4 = (f32[64,2,128]{2,0,1:T(8,128)S(1)}, f32[64,2,128]{2,0,1:T(8,128)S(1)}, u32[]{:S(2)}, u32[]{:S(2)}) collective-permute-start(f32[64,2,128]{2,0,1:T(8,128)S(1)} %get-tuple-element.26), channel_id=1, source_target_pairs={{0,8},{8,16},{16,24},{1,9},{9,17},{17,25},{2,10},{10,18},{18,26},{... | collective-permute-start | bytes 196616 | tf_op jit(solution)/shard_map/ppermute | solution.py:43
  39.2 1.5 collective-permute-start.5
  40.7 0.0 slice-done
  40.7 0.0 slice-done.1
  40.7 7.5 %multiply_reduce_fusion = (f32[1024]{0:T(1024)S(1)}, bf16[1,1024,16,128]{3,2,1,0:T(8,128)(2,1)}, bf16[1,1,1024,16,128]{4,3,0,2,1:T(8,128)(2,1)}) fusion(f32[16,128]{1,0:T(8,128)S(1)} %dynamic-slice_convert_fusion, s32[1024,16,128]{2,1,0:T(8,128)S(1)} %bitcast.21), kind=kLoop, calls=%fused_computation.4 | loop fusion | flops 14679040 | bytes 16789504 | tf_op jit(solution)/shard_map/reduce_sum | solution.py:82
  48.2 1.5 collective-permute-start.8
  49.7 0.0 collective-permute-done.4
  49.7 0.0 collective-permute-done.5
  49.7 0.1 pad_maximum_fusion.3
  49.8 0.4 fusion.13
  50.2 1.2 add_multiply_fusion.1
  51.4 0.4 fusion.17
  51.8 1.1 multiply_add_fusion
  52.9 4.5 %collective-permute-start.6 = (f32[64,2,128]{2,0,1:T(8,128)S(1)}, f32[64,2,128]{2,0,1:T(8,128)S(1)}, u32[]{:S(2)}, u32[]{:S(2)}) collective-permute-start(f32[64,2,128]{2,0,1:T(8,128)S(1)} %get-tuple-element.24), channel_id=1, source_target_pairs={{0,8},{8,16},{16,24},{1,9},{9,17},{17,25},{2,10},{10,18},{18,26},{... | collective-permute-start | bytes 196616 | tf_op jit(solution)/shard_map/ppermute | solution.py:43
  57.5 1.3 collective-permute-start.7
  58.8 0.6 collective-permute-done.6
  59.4 4.3 %collective-permute-done.7 = f32[64,2,128]{2,0,1:T(8,128)S(1)} collective-permute-done((f32[64,2,128]{2,0,1:T(8,128)S(1)}, f32[64,2,128]{2,0,1:T(8,128)S(1)}, u32[]{:S(2)}, u32[]{:S(2)}) %collective-permute-start.7) | collective-permute-done | bytes 65568 | tf_op jit(solution)/shard_map/ppermute | solution.py:44
  63.6 0.1 pad_maximum_fusion.4
  63.8 0.4 fusion.12
  64.2 1.2 add_multiply_fusion
  65.4 0.4 fusion.16
  65.8 2.0 fusion.8
  67.8 0.0 all-gather.2.cloned.1.call-update
  67.8 0.0 all-reduce.18.cloned.1.call-start
  67.9 69.9 %psum.21 = f32[1024]{0:T(1024)S(1)} all-reduce(f32[1024]{0:T(1024)S(1)} %get-tuple-element.5), channel_id=1, replica_groups=mesh['mod'=4,'frm'=2,'ori'=4] {'frm'}, use_global_device_ids=true, to_apply=%region_1.0 | all-reduce | flops 1024 | bytes 8192 | tf_op jit(solution)/shard_map/psum | solution.py:83
  137.7 0.0 collective-permute-done.8
  137.7 7.4 %pad_maximum_fusion = bf16[2,1,1024,16,128]{4,3,0,2,1:T(8,128)(2,1)} fusion(bf16[1,1,1024,16,128]{4,3,0,2,1:T(8,128)(2,1)} %bitcast.3, bf16[1,1,1024,16,128]{4,3,0,2,1:T(8,128)(2,1)} %get-tuple-element.7), kind=kLoop, calls=%fused_computation.1 | loop fusion | flops 4194304 | bytes 16777216 | tf_op jit(solution)/shard_map/stack | solution.py:26
  145.2 11.1 %reverse_select_fusion = bf16[2,1,1024,16,128]{4,3,0,2,1:T(8,128)(2,1)} fusion(bf16[2,1,1024,16,128]{4,3,0,2,1:T(8,128)(2,1)} %pad_maximum_fusion, pred[]{:T(512)S(6)} %eq.3), kind=kLoop, calls=%fused_computation | loop fusion | flops 4194304 | bytes 16777216 | tf_op jit(solution)/shard_map/jit(_where)/select_n | solution.py:28
  156.3 0.0 all-gather.2.cloned.1.call-done
  156.3 9.6 %fusion.5 = f32[256,1024]{1,0:T(8,128)} fusion(bf16[256,32,128]{2,0,1:T(8,128)(2,1)} %all-gather.2.cloned.1.call-done, bf16[1024,32,128]{2,1,0:T(8,128)(2,1)} %bitcast.19, f32[1024]{0:T(1024)S(1)} %psum.21), kind=kOutput, calls=%fused_computation.7 | convolution fusion | flops 2147745792 | bytes 11538432 | tf_op jit(solution)/shard_map/dot_general | solution.py:84
  165.9 0.0 all-reduce.18.cloned.1.call-update
  166.0 52.1 %all-reduce.18.cloned.1.call-done = f32[256,1024]{1,0:T(8,128)} async-done(((f32[256,1024]{1,0:T(8,128)}), f32[256,1024]{1,0:T(8,128)}) %all-reduce.18.cloned.1.call-update) | async-done | bytes 1048592 | tf_op jit(solution)/shard_map/psum | solution.py:92
  218.0 1.1 fusion.9
  219.1 6.9 %pmax.7 = f32[64]{0:T(128)S(1)} all-reduce(f32[64]{0:T(128)S(1)} %fusion.9), channel_id=1, replica_groups=mesh['mod'=4,'frm'=2,'ori'=4] {'ori'}, use_global_device_ids=true, to_apply=%region_4.5 | all-reduce | flops 64 | bytes 512 | tf_op jit(solution)/shard_map/pmax | solution.py:96
  226.0 1.2 exponential_reduce_fusion
  227.1 5.9 %psum.23 = f32[64]{0:T(128)S(1)} all-reduce(f32[64]{0:T(128)S(1)} %exponential_reduce_fusion), channel_id=1, replica_groups=mesh['mod'=4,'frm'=2,'ori'=4] {'ori'}, use_global_device_ids=true, to_apply=%region_6.7 | all-reduce | flops 64 | bytes 512 | tf_op jit(solution)/shard_map/psum | solution.py:97
  233.1 1.7 subtract_bitcast_fusion
  (9 shorter events, 0.1 us)
Async XLA Ops:
  6.5 149.8 %all-gather.2.cloned.1.call-start = ((), (), s32[]{:S(2)}) async-start(), calls=%async_computation | async-start | bytes 2621440 | tf_op jit(solution)/shard_map/all_gather | solution.py:76
  8.4 6.9 %collective-permute-start = (f32[64,2,128]{2,0,1:T(8,128)S(1)}, f32[64,2,128]{2,0,1:T(8,128)S(1)}, u32[]{:S(2)}, u32[]{:S(2)}) collective-permute-start(f32[64,2,128]{2,0,1:T(8,128)S(1)} %get-tuple-element.30), channel_id=1, source_target_pairs={{0,8},{8,16},{16,24},{1,9},{9,17},{17,25},{2,10},{10,18},{18,26},{... | collective-permute-start | bytes 196616 | tf_op jit(solution)/shard_map/ppermute | solution.py:43
  13.4 6.2 %collective-permute-start.1 = (f32[64,2,128]{2,0,1:T(8,128)S(1)}, f32[64,2,128]{2,0,1:T(8,128)S(1)}, u32[]{:S(2)}, u32[]{:S(2)}) collective-permute-start(f32[64,2,128]{2,0,1:T(8,128)S(1)} %get-tuple-element.31), channel_id=1, source_target_pairs={{8,0},{16,8},{24,16},{9,1},{17,9},{25,17},{10,2},{18,10},{26,18},{... | collective-permute-start | bytes 196616 | tf_op jit(solution)/shard_map/ppermute | solution.py:44
  21.6 5.9 %copy-start = (s32[32,128]{1,0:T(8,128)S(1)}, s32[32,128]{1,0:T(8,128)}, u32[]{:S(2)}) copy-start(s32[32,128]{1,0:T(8,128)} %param.5) | copy-start | bytes 49156
  22.8 5.4 %collective-permute-start.2 = (f32[64,2,128]{2,0,1:T(8,128)S(1)}, f32[64,2,128]{2,0,1:T(8,128)S(1)}, u32[]{:S(2)}, u32[]{:S(2)}) collective-permute-start(f32[64,2,128]{2,0,1:T(8,128)S(1)} %get-tuple-element.28), channel_id=1, source_target_pairs={{0,8},{8,16},{16,24},{1,9},{9,17},{17,25},{2,10},{10,18},{18,26},{... | collective-permute-start | bytes 196616 | tf_op jit(solution)/shard_map/ppermute | solution.py:43
  26.3 6.2 %collective-permute-start.3 = (f32[64,2,128]{2,0,1:T(8,128)S(1)}, f32[64,2,128]{2,0,1:T(8,128)S(1)}, u32[]{:S(2)}, u32[]{:S(2)}) collective-permute-start(f32[64,2,128]{2,0,1:T(8,128)S(1)} %get-tuple-element.29), channel_id=1, source_target_pairs={{8,0},{16,8},{24,16},{9,1},{17,9},{25,17},{10,2},{18,10},{26,18},{... | collective-permute-start | bytes 196616 | tf_op jit(solution)/shard_map/ppermute | solution.py:44
  32.9 7.8 %slice-start = ((s8[8388608]{0:T(1024)(128)(4,1)}), s8[4194304]{0:T(1024)(128)(4,1)S(1)}, s32[]{:S(2)}) async-start(s8[8388608]{0:T(1024)(128)(4,1)} %bitcast.20), calls=%async_computation.2 | async-start | bytes 8388608
  34.2 6.5 %slice-start.1 = ((s8[8388608]{0:T(1024)(128)(4,1)}), s8[4194304]{0:T(1024)(128)(4,1)S(1)}, s32[]{:S(2)}) async-start(s8[8388608]{0:T(1024)(128)(4,1)} %bitcast.20), calls=%async_computation.3 | async-start | bytes 8388608
  35.7 14.0 %collective-permute-start.4 = (f32[64,2,128]{2,0,1:T(8,128)S(1)}, f32[64,2,128]{2,0,1:T(8,128)S(1)}, u32[]{:S(2)}, u32[]{:S(2)}) collective-permute-start(f32[64,2,128]{2,0,1:T(8,128)S(1)} %get-tuple-element.26), channel_id=1, source_target_pairs={{0,8},{8,16},{16,24},{1,9},{9,17},{17,25},{2,10},{10,18},{18,26},{... | collective-permute-start | bytes 196616 | tf_op jit(solution)/shard_map/ppermute | solution.py:43
  39.2 10.5 %collective-permute-start.5 = (f32[64,2,128]{2,0,1:T(8,128)S(1)}, f32[64,2,128]{2,0,1:T(8,128)S(1)}, u32[]{:S(2)}, u32[]{:S(2)}) collective-permute-start(f32[64,2,128]{2,0,1:T(8,128)S(1)} %get-tuple-element.27), channel_id=1, source_target_pairs={{8,0},{16,8},{24,16},{9,1},{17,9},{25,17},{10,2},{18,10},{26,18},{... | collective-permute-start | bytes 196616 | tf_op jit(solution)/shard_map/ppermute | solution.py:44
  48.2 89.5 %collective-permute-start.8 = (bf16[1,1024,16,128]{3,2,1,0:T(8,128)(2,1)}, bf16[1,1024,16,128]{3,2,1,0:T(8,128)(2,1)}, u32[]{:S(2)}, u32[]{:S(2)}) collective-permute-start(bf16[1,1024,16,128]{3,2,1,0:T(8,128)(2,1)} %get-tuple-element.6), channel_id=1, source_target_pairs={{0,4},{4,0},{1,5},{5,1},{2,6},{6,2},{3,7},{7,3},{8,12},{12,8},{9,1... | collective-permute-start | bytes 12582920 | tf_op jit(solution)/shard_map/ppermute | solution.py:25
  52.9 6.4 %collective-permute-start.6 = (f32[64,2,128]{2,0,1:T(8,128)S(1)}, f32[64,2,128]{2,0,1:T(8,128)S(1)}, u32[]{:S(2)}, u32[]{:S(2)}) collective-permute-start(f32[64,2,128]{2,0,1:T(8,128)S(1)} %get-tuple-element.24), channel_id=1, source_target_pairs={{0,8},{8,16},{16,24},{1,9},{9,17},{17,25},{2,10},{10,18},{18,26},{... | collective-permute-start | bytes 196616 | tf_op jit(solution)/shard_map/ppermute | solution.py:43
  57.5 6.2 %collective-permute-start.7 = (f32[64,2,128]{2,0,1:T(8,128)S(1)}, f32[64,2,128]{2,0,1:T(8,128)S(1)}, u32[]{:S(2)}, u32[]{:S(2)}) collective-permute-start(f32[64,2,128]{2,0,1:T(8,128)S(1)} %get-tuple-element.25), channel_id=1, source_target_pairs={{8,0},{16,8},{24,16},{9,1},{17,9},{25,17},{10,2},{18,10},{26,18},{... | collective-permute-start | bytes 196616 | tf_op jit(solution)/shard_map/ppermute | solution.py:44
  67.8 150.2 %all-reduce.18.cloned.1.call-start = ((), (), s32[]{:S(2)}) async-start(), calls=%async_computation.1 | async-start | bytes 2097152 | tf_op jit(solution)/shard_map/psum | solution.py:92
Sparse Core Ops, SparseCore 0:
  67.9 19.8 all-gather.1
  166.1 51.9 all-reduce.17
